TPU v7x, 256 devices: a whole 4x4x8 slice. The times are simulated.
256 devices in a mesh: seq: 32 (over z, y), tp: 8 (over x, core).
Axes of the slice: x: 4, y: 4, z: 8, core: 2. Of those that a mesh axis runs over, the one named last changes fastest.
Arguments:
- query_rows: bfloat16 [8192, 6144], P('seq', 'tp'), may hold values from -6 to 6
- key_rows: bfloat16 [8192, 6144], P('seq', 'tp'), may hold values from -6 to 6
- value_rows: bfloat16 [8192, 6144], P('seq', 'tp'), may hold values from -81 to 81
- out_grad: bfloat16 [8192, 6144], P('seq'), may hold values from -6 to 6
- out_weight: bfloat16 [6144, 6144], P('tp', 'seq'), may hold values from -0.078125 to 0.078125
Outputs:
- query_grad: bfloat16 [8192, 6144], P('seq', 'tp')
- key_grad: bfloat16 [8192, 6144], P('seq', 'tp')
- value_grad: bfloat16 [8192, 6144], P('seq', 'tp')
- weight_grad: bfloat16 [6144, 6144], P('tp', 'seq')
All inputs are finite; a program needn't handle non-finite values.
Results may differ from a plain program's by a relative error of at most 0.025.
Values may be sent and summed in bfloat16 or wider, within the bound.
A program may use at most 128 MiB of HBM per device.

v0:
```python
import jax
import jax.numpy as jnp
from jax import lax
from jax.sharding import PartitionSpec as P

HEADS = 64
HDIM = 96


EPSILON = 1e-06
HIGHEST = lax.Precision.HIGHEST


def prefix(shard, axis, combine, identity, reverse):
    length, place = (lax.axis_size(axis), lax.axis_index(axis))
    everything = lax.all_gather(shard.astype(jnp.bfloat16), axis)
    start = jnp.broadcast_to(jnp.asarray(identity, shard.dtype), shard.shape)

    def turn(k, before):
        at = length - 1 - k if reverse else k
        reached = at > place if reverse else at < place
        new = combine(before, everything[at].astype(shard.dtype))
        return jnp.where(reached, new, before)

    return lax.fori_loop(0, length, turn, start)


def causal_mask(length):
    row_ids = lax.broadcasted_iota(jnp.int32, (length, length), 0)
    col_ids = lax.broadcasted_iota(jnp.int32, (length, length), 1)
    return (row_ids >= col_ids).astype(jnp.float32)


def add_state(first, second):
    return first + second


def body(query_rows, key_rows, value_rows, out_grad, out_weight):
    length = query_rows.shape[0]
    columns = query_rows.shape[1]
    head_count = columns // HDIM
    all_columns = HEADS * HDIM
    f32 = jnp.float32
    queries = query_rows.reshape(length, head_count, HDIM)
    keyset = key_rows.reshape(length, head_count, HDIM)
    valueset = value_rows.reshape(length, head_count, HDIM)
    causal = causal_mask(length)
    scores = (
        jnp.einsum("thd,shd->hts", queries, keyset, preferred_element_type=f32) * causal
    ).astype(jnp.bfloat16)
    local_kv = jnp.einsum("shd,she->hde", keyset, valueset, preferred_element_type=f32).reshape(
        1, -1
    )
    zeros_flat = jnp.zeros_like(local_kv)
    prefix_flat = prefix(local_kv, "seq", add_state, zeros_flat, False)
    prefix_state = prefix_flat.reshape(head_count, HDIM, HDIM)
    query_f32 = queries.astype(f32)
    attended = jnp.einsum("hts,she->the", scores, valueset, preferred_element_type=f32)
    attended = attended + jnp.einsum("thd,hde->the", query_f32, prefix_state, precision=HIGHEST)
    attended = attended.reshape(length, columns)
    grad_cols = out_grad
    normed_grad = lax.dot_general(
        grad_cols,
        lax.all_gather(out_weight, "seq", axis=1, tiled=True),
        (((1,), (1,)), ((), ())),
        preferred_element_type=f32,
    )
    square_sum, cross_sum = lax.psum(
        (jnp.sum(attended * attended, axis=1), jnp.sum(normed_grad * attended, axis=1)), "tp"
    )
    row_rms = jnp.sqrt(square_sum / all_columns + EPSILON)
    normed = attended / row_rms[:, None]
    normed_bf = normed.astype(jnp.bfloat16)
    cross = cross_sum / row_rms
    attended_grad = (
        (normed_grad - normed * (cross / all_columns)[:, None]) / row_rms[:, None]
    ).astype(jnp.bfloat16)
    grad_cols = out_grad
    weight_sum = lax.psum_scatter(
        lax.dot_general(
            grad_cols, normed_bf, (((0,), (0,)), ((), ())), preferred_element_type=f32
        ).astype(jnp.bfloat16),
        "seq",
        scatter_dimension=0,
        tiled=True,
    ).astype(jnp.float32)
    weight_grad = weight_sum.T.astype(jnp.bfloat16)
    grad_heads = attended_grad.reshape(length, head_count, HDIM)
    local_grad = jnp.einsum(
        "thd,the->hde", queries, grad_heads, preferred_element_type=f32
    ).reshape(1, -1)
    suffix_flat = prefix(local_grad, "seq", add_state, zeros_flat, True)
    suffix_state = suffix_flat.reshape(head_count, HDIM, HDIM)
    grad_f32 = grad_heads.astype(f32)
    score_grad = (
        jnp.einsum("the,she->hts", grad_heads, valueset, preferred_element_type=f32) * causal
    ).astype(jnp.bfloat16)
    query_grad = jnp.einsum("hts,shd->thd", score_grad, keyset, preferred_element_type=f32)
    query_grad = query_grad + jnp.einsum("the,hde->thd", grad_f32, prefix_state, precision=HIGHEST)
    key_grad = jnp.einsum("hts,thd->shd", score_grad, queries, preferred_element_type=f32)
    key_grad = key_grad + jnp.einsum(
        "she,hde->shd", valueset.astype(f32), suffix_state, precision=HIGHEST
    )
    value_grad = jnp.einsum("hts,the->she", scores, grad_heads, preferred_element_type=f32)
    value_grad = value_grad + jnp.einsum(
        "shd,hde->she", keyset.astype(f32), suffix_state, precision=HIGHEST
    )
    return (
        query_grad.reshape(length, columns).astype(jnp.bfloat16),
        key_grad.reshape(length, columns).astype(jnp.bfloat16),
        value_grad.reshape(length, columns).astype(jnp.bfloat16),
        weight_grad,
    )


def solution(mesh):
    placed = (P("seq", "tp"), P("seq", "tp"), P("seq", "tp"), P("seq", None), P("tp", "seq"))
    return jax.shard_map(
        body,
        mesh=mesh,
        in_specs=placed,
        out_specs=(P("seq", "tp"), P("seq", "tp"), P("seq", "tp"), P("tp", "seq")),
        check_vma=False,
    )
```

profile of v0, /device:TPU:2, one launch (start us, length us, event | category | flops | bytes accessed | tf_op | source)
XLA Modules:
  0.0 592.1 jit_solution(586325400160768626)
XLA Ops:
  8.6 2.1 copy.47
  10.6 1.9 convolution_convert_fusion.2
  12.5 1.9 convert_element_type.132
  20.6 2.4 convolution_bitcast_fusion.2
  23.0 98.1 %all-gather.6.cloned.1.call-done = bf16[32,1,73728]{2,1,0:T(2,128)(2,1)} async-done(((bf16[1,1,73728]{2,1,0:T(2,128)(2,1)}), bf16[32,1,73728]{2,1,0:T(2,128)(2,1)}) %all-gather.6.cloned.1.call-update) | async-done | bytes 4718608 | tf_op jit(solution)/shard_map/all_gather | solution.py:16
  121.1 45.3 %while.30 = (s32[]{:T(128)}, f32[1,73728]{1,0:T(1,128)S(1)}, s32[]{:T(128)}, bf16[32,1,73728]{2,1,0:T(2,128)(2,1)}, s32[]{:T(128)}, /*index=5*/s32[]{:T(128)}) while((s32[]{:T(128)}, f32[1,73728]{1,0:T(1,128)S(1)}, s32[]{:T(128)}, bf16[32,1,73728]{2,1,0:T(2,128)(2,1)}, s32[]{:T(128)}, /*index=5*/s32[]{:T(128)}) %tuple.77), condition=%wide.region_1.2_spmd.clone, body=%wide.region_0.1_spmd.clone.sunk | while | flops 294916 | bytes 737381 | solution.py:25
  167.0 2.1 reduce.7
  170.2 2.9 multiply_reduce_fusion.1
  173.1 2.3 copy.49
  175.4 49.0 %all-gather.4.cloned.1.call-done = bf16[768,6144]{0,1:T(8,128)(2,1)} async-done(((bf16[768,192]{0,1:T(8,128)(2,1)}), bf16[768,6144]{0,1:T(8,128)(2,1)}) %all-gather.4.cloned.1.call-update) | async-done | bytes 9437200 | tf_op jit(solution)/shard_map/all_gather | solution.py:64
  224.3 7.4 %multiply_reduce_fusion = (f32[256]{0:T(256)S(1)}, f32[256,768]{1,0:T(8,128)}) fusion(f32[256,768]{1,0:T(8,128)} %copy.49, bf16[256,6144]{1,0:T(8,128)(2,1)S(1)} %copy-done, bf16[768,6144]{0,1:T(8,128)(2,1)} %all-gather.4.cloned.1.call-done), kind=kOutput, calls=%fused_computation.25 | convolution fusion | flops 2416312064 | bytes 14156800 | tf_op jit(solution)/shard_map/dot_general | solution.py:62
  231.7 11.2 %all-reduce = (f32[256]{0:T(256)S(1)}, f32[256]{0:T(256)S(1)}) all-reduce(f32[256]{0:T(256)S(1)} %get-tuple-element.257, f32[256]{0:T(256)S(1)} %get-tuple-element.259), channel_id=1, replica_groups=mesh['seq'=32,'tp'=8] {'tp'}, use_global_device_ids=true, to_apply=%region_5.6 | all-reduce | flops 512 | bytes 4096 | tf_op jit(solution)/shard_map/psum | solution.py:68
  243.0 2.3 divide_convert_fusion
  245.3 1.9 copy.51
  247.2 1.9 fusion.7
  258.1 6.5 %fusion = bf16[6144,768]{0,1:T(8,128)(2,1)} fusion(bf16[256,6144]{1,0:T(8,128)(2,1)S(1)} %copy-done, f32[256,768]{1,0:T(8,128)} %copy.49, f32[256]{0:T(256)S(1)} %get-tuple-element.255), kind=kOutput, calls=%fused_computation.5 | convolution fusion | flops 2421030912 | bytes 13370368 | tf_op jit(solution)/shard_map/dot_general | solution.py:80
  264.6 12.9 %copy.60 = bf16[6144,768]{1,0:T(8,128)(2,1)} copy(bf16[6144,768]{0,1:T(8,128)(2,1)} %fusion) | data formatting | bytes 18874368
  280.0 72.5 %all-gather.8.cloned.1.call-done = bf16[32,1,73728]{2,1,0:T(2,128)(2,1)} async-done(((bf16[1,1,73728]{2,1,0:T(2,128)(2,1)}), bf16[32,1,73728]{2,1,0:T(2,128)(2,1)}) %all-gather.8.cloned.1.call-update) | async-done | bytes 4718608 | tf_op jit(solution)/shard_map/all_gather | solution.py:16
  352.5 45.5 %while.31 = (s32[]{:T(128)}, f32[1,73728]{1,0:T(1,128)S(1)}, s32[]{:T(128)}, bf16[32,1,73728]{2,1,0:T(2,128)(2,1)}, s32[]{:T(128)}, /*index=5*/s32[]{:T(128)}, s32[]{:T(128)}, s32[]{:T(128)}) while((s32[]{:T(128)}, f32[1,73728]{1,0:T(1,128)S(1)}, s32[]{:T(128)}, bf16[32,1,73728]{2,1,0:T(2,128)(2,1)}, s32[]{:T(128)}, ...), condition=%wide.region_7.8_spmd.clone, body=%wide.region_6.7_spmd.clone.sunk | while | flops 294920 | bytes 737443 | solution.py:25
  398.0 2.2 reduce.8
  402.2 2.6 fusion.5
  404.8 1.9 copy.55
  406.7 2.6 fusion.6
  411.2 174.4 %reduce-scatter.4.cloned.1.call-done = bf16[192,768]{1,0:T(8,128)(2,1)} async-done(((bf16[6144,768]{1,0:T(8,128)(2,1)}), bf16[192,768]{1,0:T(8,128)(2,1)}) %reduce-scatter.4.cloned.1.call-update) | async-done | bytes 294928
  (119 shorter events, 113.4 us)
Async XLA Ops:
  7.2 217.2 %copy-start = (bf16[256,6144]{1,0:T(8,128)(2,1)S(1)}, bf16[256,6144]{1,0:T(8,128)(2,1)}, u32[]{:S(2)}) copy-start(bf16[256,6144]{1,0:T(8,128)(2,1)} %param.12) | copy-start | bytes 9437188
  7.2 113.9 %all-gather.6.cloned.1.call-start = ((), (), s32[]{:S(2)}) async-start(), calls=%async_computation.2 | async-start | bytes 9732096 | tf_op jit(solution)/shard_map/all_gather | solution.py:16
  8.5 6.7 %copy-start.2 = (bf16[256,768]{0,1:T(8,128)(2,1)}, bf16[256,768]{0,1:T(8,128)(2,1)S(1)}, u32[]{:S(2)}) copy-start(bf16[256,768]{0,1:T(8,128)(2,1)S(1)} %copy.46) | copy-start | bytes 1179652
  14.5 209.9 %all-gather.4.cloned.1.call-start = ((), (), s32[]{:S(2)}) async-start(), calls=%async_computation.1 | async-start | bytes 9732096 | tf_op jit(solution)/shard_map/all_gather | solution.py:64
  15.2 337.3 %all-gather.8.cloned.1.call-start = ((), (), s32[]{:S(2)}) async-start(), calls=%async_computation.3 | async-start | bytes 9732096 | tf_op jit(solution)/shard_map/all_gather | solution.py:16
  19.6 1.0 copy-start.8
  170.2 2.9 copy-start.12
  175.4 71.8 %copy-start.4 = (bf16[256,768]{0,1:T(8,128)(2,1)S(1)}, bf16[256,768]{0,1:T(8,128)(2,1)}, u32[]{:S(2)}) copy-start(bf16[256,768]{0,1:T(8,128)(2,1)} %copy.45) | copy-start | bytes 1179652
  251.3 334.3 %reduce-scatter.4.cloned.1.call-start = ((), (), s32[]{:S(2)}) async-start(), calls=%async_computation.4 | async-start | bytes 9732096
  251.5 3.5 copy-start.6
  251.5 3.5 copy-start.13
  253.3 3.0 copy-start.10
  264.6 12.9 %copy-start.5 = (bf16[256,768]{0,1:T(8,128)(2,1)S(1)}, bf16[256,768]{0,1:T(8,128)(2,1)}, u32[]{:S(2)}) copy-start(bf16[256,768]{0,1:T(8,128)(2,1)} %copy.45) | copy-start | bytes 1179652
  264.6 12.9 %copy-start.11 = (bf16[8,256,256]{2,1,0:T(8,128)(2,1)S(1)}, bf16[8,256,256]{2,1,0:T(8,128)(2,1)}, u32[]{:S(2)}) copy-start(bf16[8,256,256]{2,1,0:T(8,128)(2,1)} %copy-done.10) | copy-start | bytes 3145732
  264.6 14.1 %copy-start.7 = (bf16[256,768]{0,1:T(8,128)(2,1)S(1)}, bf16[256,768]{0,1:T(8,128)(2,1)}, u32[]{:S(2)}) copy-start(bf16[256,768]{0,1:T(8,128)(2,1)} %copy.51) | copy-start | bytes 1179652
  264.6 14.1 %copy-start.9 = (bf16[8,256,256]{2,1,0:T(8,128)(2,1)S(1)}, bf16[8,256,256]{2,1,0:T(8,128)(2,1)}, u32[]{:S(2)}) copy-start(bf16[8,256,256]{2,1,0:T(8,128)(2,1)} %copy-done.8) | copy-start | bytes 3145732
  398.0 187.5 %copy-start.1 = (bf16[256,6144]{1,0:T(8,128)(2,1)S(1)}, bf16[256,6144]{1,0:T(8,128)(2,1)}, u32[]{:S(2)}) copy-start(bf16[256,6144]{1,0:T(8,128)(2,1)} %param.12) | copy-start | bytes 9437188
  400.3 6.4 %copy-start.3 = (bf16[256,768]{0,1:T(8,128)(2,1)S(1)}, bf16[256,768]{0,1:T(8,128)(2,1)}, u32[]{:S(2)}) copy-start(bf16[256,768]{0,1:T(8,128)(2,1)} %copy-done.2) | copy-start | bytes 1179652
Sparse Core Ops, SparseCore 0:
  14.6 106.4 all-gather.5
  123.7 100.5 all-gather.3
  251.4 101.1 all-gather.7
  357.0 228.5 reduce-scatter.3
where the time goes:
time: 595 us; the launch traced here: 592 us
  waiting for transfers between devices  395 us (66%)
  other arithmetic  96.5 us (16%)
  matrix products  36.9 us (6%)
  local copies, waits for them, and re-layouts  36.8 us (6%)
  between operations  13.9 us (2%)
  blocking collectives  11.2 us (2%)
    unnamed x5, waiting for transfers between devices  175 us
    all_gather x2, waiting for transfers between devices, prefix(): everything = lax.all_gather(shard.astype(jnp.bfloat16), axis)  171 us
    select_n x64, other arithmetic, turn(): return jnp.where(reached, new, before)  89.1 us
    all_gather x1, waiting for transfers between devices, body(): lax.all_gather(out_weight, 'seq', axis=1, tiled=True)  49 us
    unnamed x35, local copies, waits for them, and re-layouts  25 us
  transfers between devices with their start and end apart: 4, of which 4 were waited for; matrix products, arithmetic and copies ran while one was open for 25% of the time, Pallas kernels for 0%

commit v1 on v0

v1 whole, which is shorter than its diff:
```python
import jax
import jax.numpy as jnp
from jax import lax
from jax.experimental import pallas as pl
from jax.experimental.pallas import tpu as pltpu
from jax.sharding import PartitionSpec as P

HDIM = 96
EPSILON = 1e-06
NY, NZ, NT = 4, 8, 8
TOK = 256
COLS = 768
GROUP = 384
CHUNK = 192
HALF = 96
QUARTER = 48
MODEL = 6144
WINDOWS = ((0, 128), (0, 256), (128, 384), (256, 384))
SEMS = 120
F32 = jnp.float32
BF16 = jnp.bfloat16


def dot(a, b, ca, cb):
    return lax.dot_general(a, b, (((ca,), (cb,)), ((), ())), preferred_element_type=F32)


def head_mask(h, lo, hi):
    lane = lax.broadcasted_iota(jnp.int32, (1, hi - lo), 1) + lo
    inside = (lane >= HDIM * h) & (lane < HDIM * (h + 1))
    return jnp.where(inside, 1.0, 0.0).astype(F32)


def kernel(
    q, k, v, w, og, qg, kg, vg, dw,
    grads, weights, normed, scores, att, ng, part, psend, precv, hsend, hrecv,
    lstate, lrecv, tsend, trecv, tacc, pfs, state, blocks, ssend, srecv,
    own, dsend, drecv, dob, gh, send, recv, lsem,
):
    s, t = lax.axis_index("seq"), lax.axis_index("tp")
    z, y = s // NY, s % NY
    core = t % 2
    odd = y % 2
    right, left, twin = (t + 2) % NT, (t + NT - 2) % NT, t + 1 - 2 * core
    count = [0]
    started = []

    def along_y(d):
        return z * NY + (y + d) % NY

    def along_z(d):
        return ((z + d + NZ) % NZ) * NY + y

    def copy(src, dst, seq, tp):
        i = count[0]
        count[0] += 1
        return pltpu.make_async_remote_copy(
            src_ref=src, dst_ref=dst, send_sem=send.at[i], recv_sem=recv.at[i],
            device_id={"seq": seq, "tp": tp}, device_id_type=pl.DeviceIdType.MESH,
        )

    def go(c):
        c.start()
        started.append(c)

    barrier = pltpu.get_barrier_semaphore()
    peers = [(along_y(d), t) for d in range(1, NY)]
    peers += [(along_z(d), t) for d in range(1, NZ)]
    peers += [(s, (t + d) % NT) for d in range(1, NT)]
    for seq, tp in peers:
        pl.semaphore_signal(
            barrier, inc=1, device_id={"seq": seq, "tp": tp}, device_id_type=pl.DeviceIdType.MESH
        )

    def window(at_z, at_y):
        return pl.multiple_of(COLS * at_z + GROUP * (at_y // 2) + 128 * (at_y % 2), 128)

    own_grads = []
    for j in range(NZ):
        c = pltpu.make_async_copy(
            og.at[:, pl.ds(window(j, y), 256)],
            grads.at[pl.ds(0, TOK), pl.ds(256 * j, 256)],
            lsem.at[j],
        )
        c.start()
        own_grads.append(c)

    for j in range(NZ):
        pad = pl.multiple_of(256 * j + CHUNK * (1 - odd), 64)
        weights[pl.ds(pad, 64), :] = jnp.zeros((64, COLS), BF16)

    def weight_rows(j, h, n):
        return pl.ds(pl.multiple_of(256 * j + 64 * odd + HALF * h, 32), n)

    weights[weight_rows(z, 0, CHUNK), :] = w[...].T

    pl.semaphore_wait(barrier, len(peers))

    wcopy = {}
    for step in range(4):
        for way in (0, 1):
            j = (z + NZ - step) % NZ if way == 0 else (z + step) % NZ
            for h in (0, 1):
                if step < 3 or h == way:
                    rows = weight_rows(j, h, HALF)
                    wcopy[step, way, h] = copy(
                        weights.at[rows], weights.at[rows], along_z(1 - 2 * way), t
                    )
    acopy = {}
    for d in range(1, NY):
        acopy[d] = copy(
            og.at[:, pl.ds(window(t, (y + d) % NY), 256)],
            grads.at[pl.ds(TOK * (NY - d), TOK), pl.ds(pl.multiple_of(256 * t, 256), 256)],
            along_y(d), t,
        )
    bcopy = {}
    for r in range(1, NY):
        def piece(at_t, half=None):
            rows = pl.ds(TOK * r, TOK) if half is None else pl.ds(TOK * r + 128 * half, 128)
            return grads.at[rows, pl.ds(pl.multiple_of(256 * at_t, 256), 256)]

        for name, tp, at_t, half in (
            ("right", right, t, None),
            ("left", left, t, None),
            ("twin", twin, t, None),
            ("far_right", right, left, 0),
            ("far_left", left, right, 1),
            ("twin_left", twin, left, None),
            ("twin_right", twin, right, None),
            ("twin_far0", twin, (t + 4) % NT, 0),
            ("twin_far1", twin, (t + 4) % NT, 1),
        ):
            bcopy[r, name] = copy(piece(at_t, half), piece(at_t, half), s, tp)

    for h in (0, 1):
        for way in (0, 1):
            go(wcopy[0, way, h])
    for d in range(1, NY):
        go(acopy[d])

    def weight_step(step):
        for h in (0, 1):
            for way in (0, 1):
                if (step, way, h) in wcopy:
                    wcopy[step, way, h].wait_recv()
                    if (step + 1, way, h) in wcopy:
                        go(wcopy[step + 1, way, h])

    def local_state(a, b, slot):
        for g in range(2):
            full = dot(a[:, GROUP * g : GROUP * (g + 1)], b[:, GROUP * g : GROUP * (g + 1)], 0, 0)
            kept = jnp.zeros((HDIM, GROUP), F32)
            for h in range(4):
                kept = kept + full[HDIM * h : HDIM * (h + 1), :] * head_mask(h, 0, GROUP)
            lstate[slot, HDIM * g : HDIM * (g + 1), :] = kept.astype(BF16)

    states = []
    for slot in (0, 1):
        sign = 1 - 2 * slot
        first = [
            copy(
                lstate.at[slot, pl.ds(pl.multiple_of(QUARTER * ((y + d) % NY), 16), QUARTER)],
                lrecv.at[slot, y], along_y(d), t,
            )
            for d in range(1, NY)
        ]
        second = [
            copy(tsend.at[slot], trecv.at[slot, z], along_z(sign * d), t) for d in range(1, NZ)
        ]
        third = [
            copy(
                pfs.at[slot, (y + d) % NY],
                state.at[slot, pl.ds(pl.multiple_of(QUARTER * y, 16), QUARTER)],
                along_y(d), t,
            )
            for d in range(1, NY)
        ]
        states.append((first, second, third))

    def state_first(slot):
        for c in states[slot][0]:
            go(c)
        mine = pl.ds(pl.multiple_of(QUARTER * y, 16), QUARTER)
        lrecv[slot, y] = lstate[slot, mine, :]

    def state_second(slot):
        for c in states[slot][0]:
            c.wait_recv()
        total = lrecv[slot, 0].astype(F32)
        for j in range(1, NY):
            total = total + lrecv[slot, j].astype(F32)
        tsend[slot] = total.astype(BF16)
        for d in range(1, NZ):
            reaches = z + d < NZ if slot == 0 else z >= d

            @pl.when(reaches)
            def _():
                states[slot][1][d - 1].start()

    def state_third(slot):
        tacc[...] = jnp.zeros((QUARTER, GROUP), F32)
        for d in range(1, NZ):
            comes = z >= d if slot == 0 else z + d < NZ
            source = z - d if slot == 0 else z + d

            @pl.when(comes)
            def _():
                states[slot][1][d - 1].wait_recv()
                tacc[...] += trecv[slot, source].astype(F32)

        running = tacc[...]
        for j in range(NY) if slot == 0 else reversed(range(NY)):
            pfs[slot, j] = running.astype(BF16)
            running = running + lrecv[slot, j].astype(F32)
        for c in states[slot][2]:
            go(c)
        mine = pl.ds(pl.multiple_of(QUARTER * y, 16), QUARTER)
        state[slot, mine, :] = pfs[slot, y]

    def state_last(slot):
        for c in states[slot][2]:
            c.wait_recv()
        for g in range(2):
            compact = state[slot, HDIM * g : HDIM * (g + 1), :]
            for h in range(4):
                blocks[slot, g, HDIM * h : HDIM * (h + 1), :] = compact * head_mask(
                    h, 0, GROUP
                ).astype(BF16)

    sums = [
        [copy(ssend.at[i], srecv.at[i, d - 1], s, (t + d) % NT) for d in range(1, NT)]
        for i in range(2)
    ]

    def sum_send(i, column):
        ssend[i] = jnp.broadcast_to(column, (TOK, 128)).T[:8]
        for c in sums[i]:
            go(c)

    def sum_wait(i):
        total = ssend[i]
        for d in range(1, NT):
            sums[i][d - 1].wait_recv()
            total = total + srecv[i, d - 1]
        return jnp.broadcast_to(total[:1], (128, TOK)).T[:, :1]

    local_state(k, v, 0)
    state_first(0)

    rows = lax.broadcasted_iota(jnp.int32, (TOK, TOK), 0)
    columns = lax.broadcasted_iota(jnp.int32, (TOK, TOK), 1)

    def lanes(g, lo, hi):
        return pl.ds(pl.multiple_of(GROUP * g + lo, 128), hi - lo)

    def forward(g):
        att[:, lanes(g, 0, GROUP)] = jnp.zeros((TOK, GROUP), F32)
        for h, (lo, hi) in enumerate(WINDOWS):
            mask = head_mask(h, lo, hi).astype(BF16)
            at = lanes(g, lo, hi)
            score = dot(q[:, at], k[:, at] * mask, 1, 1)
            score = jnp.where(rows >= columns, score, 0.0).astype(BF16)
            scores[4 * g + h] = score
            att[:, at] += dot(score, v[:, at] * mask, 1, 0)

    forward(0)
    state_second(0)
    weight_step(0)
    for d in range(1, NY):
        acopy[d].wait_recv()
        for name in ("right", "left", "twin"):
            go(bcopy[NY - d, name])
    forward(1)
    state_third(0)
    weight_step(1)
    for r in range(1, NY):
        bcopy[r, "right"].wait_recv()
        go(bcopy[r, "far_right"])
        go(bcopy[r, "twin_left"])
        bcopy[r, "left"].wait_recv()
        go(bcopy[r, "far_left"])
        go(bcopy[r, "twin_right"])
    state_last(0)
    for g in range(2):
        at = lanes(g, 0, GROUP)
        att[:, at] += dot(q[:, at], blocks[0, g], 1, 0)
    attended = att[...]
    sum_send(0, jnp.sum(attended * attended, axis=1, keepdims=True))
    weight_step(2)
    for r in range(1, NY):
        bcopy[r, "far_right"].wait_recv()
        go(bcopy[r, "twin_far0"])
        bcopy[r, "far_left"].wait_recv()
        go(bcopy[r, "twin_far1"])
    inverse = 1.0 / jnp.sqrt(sum_wait(0) / MODEL + EPSILON)
    normed[pl.ds(0, TOK), :] = (att[...] * inverse).astype(BF16)

    ncopy = {
        "up": copy(normed.at[pl.ds(0, TOK)], normed.at[pl.ds(3 * TOK, TOK)], along_y(1), t),
        "down": copy(normed.at[pl.ds(0, TOK)], normed.at[pl.ds(TOK, TOK)], along_y(3), t),
        "far_up": copy(
            normed.at[pl.ds(3 * TOK, 128)], normed.at[pl.ds(2 * TOK, 128)], along_y(1), t
        ),
        "far_down": copy(
            normed.at[pl.ds(TOK + 128, 128)], normed.at[pl.ds(2 * TOK + 128, 128)], along_y(3), t
        ),
    }
    go(ncopy["up"])
    go(ncopy["down"])

    weight_step(3)
    for name in ("twin", "twin_left", "twin_right", "twin_far0", "twin_far1"):
        for r in range(1, NY):
            bcopy[r, name].wait_recv()
    for c in own_grads:
        c.wait()

    def product(r):
        @pl.loop(0, 3)
        def _(n):
            at = pl.ds(pl.multiple_of(256 * n, 256), 256)
            part[:, at] = dot(grads[pl.ds(TOK * r, TOK), :], weights[:, at], 1, 0)

    half_up = copy(hsend.at[pl.ds(0, 128)], hrecv.at[0], along_y(1), t)
    half_down = copy(hsend.at[pl.ds(128, 128)], hrecv.at[1], along_y(3), t)
    product(2)
    hsend[...] = part[...].astype(BF16)
    go(half_up)
    go(half_down)
    pcopy = {}
    for i, d in enumerate((1, 3)):
        for h in (0, 1):
            at = pl.ds(128 * h, 128)
            pcopy[i, h] = copy(psend.at[i, at], precv.at[i, at], along_y(d), t)
    product(1)
    psend[0, 128:] = part[128:].astype(BF16)
    go(pcopy[0, 1])
    half_up.wait_recv()
    psend[0, :128] = (part[:128] + hrecv[0].astype(F32)).astype(BF16)
    go(pcopy[0, 0])
    product(3)
    psend[1, :128] = part[:128].astype(BF16)
    go(pcopy[1, 0])
    half_down.wait_recv()
    psend[1, 128:] = (part[128:] + hrecv[1].astype(F32)).astype(BF16)
    go(pcopy[1, 1])
    ncopy["up"].wait_recv()
    go(ncopy["far_up"])
    ncopy["down"].wait_recv()
    go(ncopy["far_down"])
    product(0)

    def chunk(off):
        j = (z + off) % NZ
        turned = grads[:, pl.ds(pl.multiple_of(256 * j, 256), 256)].T
        dob[...] = turned

        @pl.loop(0, 3)
        def _(n):
            at = pl.ds(pl.multiple_of(256 * n, 256), 256)
            own[off, :, at] = dot(dob[...], normed[:, at], 1, 0)

    def valid(off, h):
        return own[off, pl.ds(pl.multiple_of(64 * odd + HALF * h, 32), HALF), :]

    dcopy = {}
    for step in range(4):
        for way in (0, 1):
            for h in (0, 1):
                if step > 0 or h == way:
                    at = pl.ds(HALF * h, HALF)
                    dcopy[step, way, h] = copy(
                        dsend.at[way, step, at], drecv.at[way, step, at],
                        along_z(2 * way - 1), t,
                    )

    ncopy["far_up"].wait_recv()
    ncopy["far_down"].wait_recv()
    chunk(4)
    for way in (0, 1):
        dsend[way, 0, HALF * way : HALF * (way + 1), :] = valid(4, way).astype(BF16)
        go(dcopy[0, way, way])

    @pl.loop(0, 7)
    def _(i):
        e = i % 2
        chunk((1 - e) * (3 - i // 2) + e * (5 + i // 2))

    def grad_step(step):
        for h in (0, 1):
            for way in (0, 1):
                off = NZ - 4 + step if way == 0 else 4 - step
                total = valid(off, h)
                if (step - 1, way, h) in dcopy:
                    dcopy[step - 1, way, h].wait_recv()
                    got = drecv[way, step - 1, HALF * h : HALF * (h + 1), :]
                    total = total + got.astype(F32)
                dsend[way, step, HALF * h : HALF * (h + 1), :] = total.astype(BF16)
                go(dcopy[step, way, h])

    for c in pcopy.values():
        c.wait_recv()
    ng[...] = part[...] + precv[0].astype(F32) + precv[1].astype(F32)
    sum_send(1, jnp.sum(ng[...] * att[...], axis=1, keepdims=True))
    grad_step(1)
    cross = sum_wait(1) * inverse
    grad_heads = (ng[...] - att[...] * (inverse * cross / MODEL)) * inverse
    gh[...] = grad_heads.astype(BF16)
    local_state(q, gh, 1)
    state_first(1)

    def backward(g):
        at = lanes(g, 0, GROUP)
        att[:, at] = dot(gh[:, at], blocks[0, g], 1, 1)
        part[:, at] = jnp.zeros((TOK, GROUP), F32)
        ng[:, at] = jnp.zeros((TOK, GROUP), F32)
        for h, (lo, hi) in enumerate(WINDOWS):
            mask = head_mask(h, lo, hi).astype(BF16)
            at = lanes(g, lo, hi)
            score = dot(gh[:, at], v[:, at] * mask, 1, 1)
            score = jnp.where(rows >= columns, score, 0.0).astype(BF16)
            att[:, at] += dot(score, k[:, at] * mask, 1, 0)
            part[:, at] += dot(score, q[:, at] * mask, 0, 0)
            ng[:, at] += dot(scores[4 * g + h], gh[:, at] * mask, 0, 0)

    backward(0)
    state_second(1)
    grad_step(2)
    backward(1)
    qg[...] = att[...].astype(BF16)
    state_third(1)
    grad_step(3)
    state_last(1)
    for g in range(2):
        at = lanes(g, 0, GROUP)
        kg[:, at] = (part[:, at] + dot(v[:, at], blocks[1, g], 1, 1)).astype(BF16)
        vg[:, at] = (ng[:, at] + dot(k[:, at], blocks[1, g], 1, 0)).astype(BF16)
    for h in (0, 1):
        for way in (0, 1):
            dcopy[3, way, h].wait_recv()
        at = slice(HALF * h, HALF * (h + 1))
        total = valid(0, h) + drecv[0, 3, at, :].astype(F32) + drecv[1, 3, at, :].astype(F32)
        own[1, at, :] = total
    dw[...] = own[1, :CHUNK, :].T.astype(BF16)

    for c in started:
        c.wait_send()
    for slot in (0, 1):
        for d in range(1, NZ):
            reaches = z + d < NZ if slot == 0 else z >= d

            @pl.when(reaches)
            def _():
                states[slot][1][d - 1].wait_send()


def body(*args):
    vmem = pl.BlockSpec(memory_space=pltpu.VMEM)
    block = jax.ShapeDtypeStruct((TOK, COLS), BF16)
    return pl.pallas_call(
        kernel,
        out_shape=(block, block, block, jax.ShapeDtypeStruct((COLS, CHUNK), BF16)),
        in_specs=[vmem] * 4 + [pl.BlockSpec(memory_space=pl.ANY)],
        out_specs=(vmem,) * 4,
        scratch_shapes=[
            pltpu.VMEM((NY * TOK, NZ * 256), BF16),
            pltpu.VMEM((NZ * 256, COLS), BF16),
            pltpu.VMEM((NY * TOK, COLS), BF16),
            pltpu.VMEM((8, TOK, TOK), BF16),
            pltpu.VMEM((TOK, COLS), F32),
            pltpu.VMEM((TOK, COLS), F32),
            pltpu.VMEM((TOK, COLS), F32),
            pltpu.VMEM((2, TOK, COLS), BF16),
            pltpu.VMEM((2, TOK, COLS), BF16),
            pltpu.VMEM((TOK, COLS), BF16),
            pltpu.VMEM((2, 128, COLS), BF16),
            pltpu.VMEM((2, 192, GROUP), BF16),
            pltpu.VMEM((2, NY, QUARTER, GROUP), BF16),
            pltpu.VMEM((2, QUARTER, GROUP), BF16),
            pltpu.VMEM((2, NZ, QUARTER, GROUP), BF16),
            pltpu.VMEM((QUARTER, GROUP), F32),
            pltpu.VMEM((2, NY, QUARTER, GROUP), BF16),
            pltpu.VMEM((2, 192, GROUP), BF16),
            pltpu.VMEM((2, 2, GROUP, GROUP), BF16),
            pltpu.VMEM((2, 8, TOK), F32),
            pltpu.VMEM((2, NT - 1, 8, TOK), F32),
            pltpu.VMEM((NZ, 256, COLS), F32),
            pltpu.VMEM((2, 4, CHUNK, COLS), BF16),
            pltpu.VMEM((2, 4, CHUNK, COLS), BF16),
            pltpu.VMEM((256, NY * TOK), BF16),
            pltpu.VMEM((TOK, COLS), BF16),
            pltpu.SemaphoreType.DMA((SEMS,)),
            pltpu.SemaphoreType.DMA((SEMS,)),
            pltpu.SemaphoreType.DMA((NZ,)),
        ],
        compiler_params=pltpu.CompilerParams(
            collective_id=0, has_side_effects=True, vmem_limit_bytes=56 << 20
        ),
    )(*args)


def solution(mesh):
    placed = (P("seq", "tp"), P("seq", "tp"), P("seq", "tp"), P("seq", None), P("tp", "seq"))
    inner = jax.shard_map(
        lambda q, k, v, og, w: body(q, k, v, w, og),
        mesh=mesh,
        in_specs=placed,
        out_specs=(P("seq", "tp"), P("seq", "tp"), P("seq", "tp"), P("tp", "seq")),
        check_vma=False,
    )
    return inner
```

time: 595 us -> 122 us (0.21)
  waiting for transfers between devices: 395 us -> 0 us
  Pallas kernels: 0 us -> 112 us
  other arithmetic: 96.5 us -> 0 us
  matrix products: 36.9 us -> 0 us
  local copies, waits for them, and re-layouts: 36.8 us -> 9.04 us
  between operations: 13.9 us -> 0.64 us
  blocking collectives: 11.2 us -> 0 us
    all_gather x3 -> x0, waiting for transfers between devices: 220 us -> none  [the longest x2 171 us: prefix(): everything = lax.all_gather(shard.astype(jnp.bfloat16), axis)]
    unnamed x5 -> x0, waiting for transfers between devices: 175 us -> none
    pallas_call x0 -> x1, Pallas kernels: none -> 112 us  [body(): pl.pallas_call(kernel, out_shape=(block, block, block, jax.ShapeDtypeStru...]
    select_n x64 -> x0, other arithmetic: 89.1 us -> none  [turn(): return jnp.where(reached, new, before)]
    dot_general x14 -> x0, matrix products: 36.9 us -> none  [the longest x1 7.4 us: body(): lax.dot_general(grad_cols, lax.all_gather(out_weight, 'seq', axis=1, tile...]
    unnamed x35 -> x4, local copies, waits for them, and re-layouts: 25 us -> 7.18 us
    psum x1 -> x0, blocking collectives: 11.2 us -> none  [body(): lax.psum((jnp.sum(attended * attended, axis=1), jnp.sum(normed_grad * att...]
  transfers between devices with their start and end apart: 4 -> 0, of which waited for: 4 -> 0; matrix products, arithmetic and copies ran while one was open for 25% -> 0% of each run, Pallas kernels for 0% -> 0%
where the time goes in v1:
time: 122 us
  Pallas kernels  112 us (92%)
  local copies, waits for them, and re-layouts  9.04 us (7%)
    pallas_call x1, Pallas kernels, body(): pl.pallas_call(kernel, out_shape=(block, block, block, jax.ShapeDtypeStru...  112 us
    unnamed x4, local copies, waits for them, and re-layouts  7.18 us

profile of v1, /device:TPU:2, one launch (start us, length us, event | category | flops | bytes accessed | tf_op | source)
XLA Modules:
  0.0 121.9 jit_solution(4343173511830258253)
XLA Ops:
  0.6 1.9 %copy.9.w = bf16[768,192]{1,0:T(8,128)(2,1)} copy(bf16[768,192]{0,1:T(8,128)(2,1)} %param.9) | data formatting | bytes 589824 | tf_op args[4]
  2.5 112.2 %shard_map.84 = (bf16[256,768]{1,0:T(8,128)(2,1)}, bf16[256,768]{1,0:T(8,128)(2,1)}, bf16[256,768]{1,0:T(8,128)(2,1)}, bf16[768,192]{1,0:T(8,128)(2,1)}) custom-call(bf16[256,768]{1,0:T(8,128)(2,1)} %q.1, bf16[256,768]{1,0:T(8,128)(2,1)} %k.1, bf16[256,768]{1,0:T(8,128)(2,1)} %v.1, bf16[768,192]{1,0:T(8,128)(2,1)} %copy.9.w, bf16[256,6144]{1,0:T(8,128)(2,1)} %og.1), custom_call_target="tpu_custom_call" | custom-call | tf_op jit(solution)/shard_map/pallas_call | solution.py:460
  114.7 1.9 %copy.10 = bf16[768,192]{0,1:T(8,128)(2,1)} copy(bf16[768,192]{1,0:T(8,128)(2,1)} %get-tuple-element.7) | data formatting | bytes 589824 | tf_op jit(solution)/shard_map/pallas_call | solution.py:460
  116.6 1.8 %copy.14 = bf16[256,768]{1,0:T(8,128)(2,1)} copy(bf16[256,768]{1,0:T(8,128)(2,1)} %get-tuple-element.12) | data formatting | bytes 786432
  118.3 1.8 %copy.15 = bf16[256,768]{1,0:T(8,128)(2,1)} copy(bf16[256,768]{1,0:T(8,128)(2,1)} %get-tuple-element.13) | data formatting | bytes 786432
  120.1 1.8 %copy.16 = bf16[256,768]{1,0:T(8,128)(2,1)} copy(bf16[256,768]{1,0:T(8,128)(2,1)} %get-tuple-element.14) | data formatting | bytes 786432

commit v2 on v1

--- a/solution.py
+++ b/solution.py
@@ -35,7 +35,7 @@
     q, k, v, w, og, qg, kg, vg, dw,
     grads, weights, normed, scores, att, ng, part, psend, precv, hsend, hrecv,
     lstate, lrecv, tsend, trecv, tacc, pfs, state, blocks, ssend, srecv,
-    own, dsend, drecv, dob, gh, send, recv, lsem,
+    own, dsend, drecv, turned, gh, held, send, recv, lsem,
 ):
     s, t = lax.axis_index("seq"), lax.axis_index("tp")
     z, y = s // NY, s % NY
@@ -92,9 +92,7 @@
     def weight_rows(j, h, n):
         return pl.ds(pl.multiple_of(256 * j + 64 * odd + HALF * h, 32), n)
 
-    weights[weight_rows(z, 0, CHUNK), :] = w[...].T
-
-    pl.semaphore_wait(barrier, len(peers))
+    weights[weight_rows(z, 0, CHUNK), :] = w[...]
 
     wcopy = {}
     for step in range(4):
@@ -132,15 +130,10 @@
         ):
             bcopy[r, name] = copy(piece(at_t, half), piece(at_t, half), s, tp)
 
-    for h in (0, 1):
-        for way in (0, 1):
-            go(wcopy[0, way, h])
-    for d in range(1, NY):
-        go(acopy[d])
-
     def weight_step(step):
-        for h in (0, 1):
+        for turn in (0, 1):
             for way in (0, 1):
+                h = way ^ turn
                 if (step, way, h) in wcopy:
                     wcopy[step, way, h].wait_recv()
                     if (step + 1, way, h) in wcopy:
@@ -245,7 +238,13 @@
         return jnp.broadcast_to(total[:1], (128, TOK)).T[:, :1]
 
     local_state(k, v, 0)
+    pl.semaphore_wait(barrier, len(peers))
     state_first(0)
+    for turn in (0, 1):
+        for way in (0, 1):
+            go(wcopy[0, way, way ^ turn])
+    for d in range(1, NY):
+        go(acopy[d])
 
     rows = lax.broadcasted_iota(jnp.int32, (TOK, TOK), 0)
     columns = lax.broadcasted_iota(jnp.int32, (TOK, TOK), 1)
@@ -273,6 +272,12 @@
     forward(1)
     state_third(0)
     weight_step(1)
+    state_last(0)
+    for g in range(2):
+        at = lanes(g, 0, GROUP)
+        att[:, at] += dot(q[:, at], blocks[0, g], 1, 0)
+    attended = att[...]
+    sum_send(0, jnp.sum(attended * attended, axis=1, keepdims=True))
     for r in range(1, NY):
         bcopy[r, "right"].wait_recv()
         go(bcopy[r, "far_right"])
@@ -280,18 +285,6 @@
         bcopy[r, "left"].wait_recv()
         go(bcopy[r, "far_left"])
         go(bcopy[r, "twin_right"])
-    state_last(0)
-    for g in range(2):
-        at = lanes(g, 0, GROUP)
-        att[:, at] += dot(q[:, at], blocks[0, g], 1, 0)
-    attended = att[...]
-    sum_send(0, jnp.sum(attended * attended, axis=1, keepdims=True))
-    weight_step(2)
-    for r in range(1, NY):
-        bcopy[r, "far_right"].wait_recv()
-        go(bcopy[r, "twin_far0"])
-        bcopy[r, "far_left"].wait_recv()
-        go(bcopy[r, "twin_far1"])
     inverse = 1.0 / jnp.sqrt(sum_wait(0) / MODEL + EPSILON)
     normed[pl.ds(0, TOK), :] = (att[...] * inverse).astype(BF16)
 
@@ -307,7 +300,12 @@
     }
     go(ncopy["up"])
     go(ncopy["down"])
-
+    weight_step(2)
+    for r in range(1, NY):
+        bcopy[r, "far_right"].wait_recv()
+        go(bcopy[r, "twin_far0"])
+        bcopy[r, "far_left"].wait_recv()
+        go(bcopy[r, "twin_far1"])
     weight_step(3)
     for name in ("twin", "twin_left", "twin_right", "twin_far0", "twin_far1"):
         for r in range(1, NY):
@@ -323,42 +321,20 @@
 
     half_up = copy(hsend.at[pl.ds(0, 128)], hrecv.at[0], along_y(1), t)
     half_down = copy(hsend.at[pl.ds(128, 128)], hrecv.at[1], along_y(3), t)
-    product(2)
-    hsend[...] = part[...].astype(BF16)
-    go(half_up)
-    go(half_down)
     pcopy = {}
     for i, d in enumerate((1, 3)):
         for h in (0, 1):
             at = pl.ds(128 * h, 128)
             pcopy[i, h] = copy(psend.at[i, at], precv.at[i, at], along_y(d), t)
-    product(1)
-    psend[0, 128:] = part[128:].astype(BF16)
-    go(pcopy[0, 1])
-    half_up.wait_recv()
-    psend[0, :128] = (part[:128] + hrecv[0].astype(F32)).astype(BF16)
-    go(pcopy[0, 0])
-    product(3)
-    psend[1, :128] = part[:128].astype(BF16)
-    go(pcopy[1, 0])
-    half_down.wait_recv()
-    psend[1, 128:] = (part[128:] + hrecv[1].astype(F32)).astype(BF16)
-    go(pcopy[1, 1])
-    ncopy["up"].wait_recv()
-    go(ncopy["far_up"])
-    ncopy["down"].wait_recv()
-    go(ncopy["far_down"])
-    product(0)
 
     def chunk(off):
         j = (z + off) % NZ
-        turned = grads[:, pl.ds(pl.multiple_of(256 * j, 256), 256)].T
-        dob[...] = turned
+        turned[...] = grads[:, pl.ds(pl.multiple_of(256 * j, 256), 256)].T
 
         @pl.loop(0, 3)
         def _(n):
             at = pl.ds(pl.multiple_of(256 * n, 256), 256)
-            own[off, :, at] = dot(dob[...], normed[:, at], 1, 0)
+            own[off, :, at] = dot(turned[...], normed[:, at], 1, 0)
 
     def valid(off, h):
         return own[off, pl.ds(pl.multiple_of(64 * odd + HALF * h, 32), HALF), :]
@@ -374,35 +350,65 @@
                         along_z(2 * way - 1), t,
                     )
 
+    def grad_half(step, turn):
+        for way in (0, 1):
+            h = way ^ (1 - turn)
+            if (step, way, h) not in dcopy:
+                continue
+            off = 4 + step if way == 0 else 4 - step
+            total = valid(off, h)
+            if (step - 1, way, h) in dcopy:
+                dcopy[step - 1, way, h].wait_recv()
+                total = total + drecv[way, step - 1, HALF * h : HALF * (h + 1), :].astype(F32)
+            dsend[way, step, HALF * h : HALF * (h + 1), :] = total.astype(BF16)
+            go(dcopy[step, way, h])
+
+    ncopy["up"].wait_recv()
+    go(ncopy["far_up"])
+    ncopy["down"].wait_recv()
+    go(ncopy["far_down"])
+    product(2)
+    hsend[...] = part[...].astype(BF16)
+    go(half_up)
+    go(half_down)
+    product(1)
+    psend[0, 128:] = part[128:].astype(BF16)
+    go(pcopy[0, 1])
+    held[0] = part[:128]
+    product(3)
+    psend[1, :128] = part[:128].astype(BF16)
+    go(pcopy[1, 0])
+    held[1] = part[128:]
     ncopy["far_up"].wait_recv()
     ncopy["far_down"].wait_recv()
     chunk(4)
-    for way in (0, 1):
-        dsend[way, 0, HALF * way : HALF * (way + 1), :] = valid(4, way).astype(BF16)
-        go(dcopy[0, way, way])
-
-    @pl.loop(0, 7)
+    grad_half(0, 1)
+
+    @pl.loop(0, 2)
+    def _(i):
+        chunk(5 - 2 * i)
+
+    grad_half(1, 0)
+    half_up.wait_recv()
+    psend[0, :128] = (held[0] + hrecv[0].astype(F32)).astype(BF16)
+    go(pcopy[0, 0])
+    half_down.wait_recv()
+    psend[1, 128:] = (held[1] + hrecv[1].astype(F32)).astype(BF16)
+    go(pcopy[1, 1])
+    grad_half(1, 1)
+    product(0)
+
+    @pl.loop(0, 5)
     def _(i):
         e = i % 2
-        chunk((1 - e) * (3 - i // 2) + e * (5 + i // 2))
-
-    def grad_step(step):
-        for h in (0, 1):
-            for way in (0, 1):
-                off = NZ - 4 + step if way == 0 else 4 - step
-                total = valid(off, h)
-                if (step - 1, way, h) in dcopy:
-                    dcopy[step - 1, way, h].wait_recv()
-                    got = drecv[way, step - 1, HALF * h : HALF * (h + 1), :]
-                    total = total + got.astype(F32)
-                dsend[way, step, HALF * h : HALF * (h + 1), :] = total.astype(BF16)
-                go(dcopy[step, way, h])
-
+        chunk((1 - e) * ((6 + i // 2) % NZ) + e * (2 - i // 2))
+
+    grad_half(2, 0)
     for c in pcopy.values():
         c.wait_recv()
     ng[...] = part[...] + precv[0].astype(F32) + precv[1].astype(F32)
     sum_send(1, jnp.sum(ng[...] * att[...], axis=1, keepdims=True))
-    grad_step(1)
+    grad_half(2, 1)
     cross = sum_wait(1) * inverse
     grad_heads = (ng[...] - att[...] * (inverse * cross / MODEL)) * inverse
     gh[...] = grad_heads.astype(BF16)
@@ -425,11 +431,11 @@
 
     backward(0)
     state_second(1)
-    grad_step(2)
+    grad_half(3, 0)
     backward(1)
     qg[...] = att[...].astype(BF16)
     state_third(1)
-    grad_step(3)
+    grad_half(3, 1)
     state_last(1)
     for g in range(2):
         at = lanes(g, 0, GROUP)
@@ -440,8 +446,7 @@
             dcopy[3, way, h].wait_recv()
         at = slice(HALF * h, HALF * (h + 1))
         total = valid(0, h) + drecv[0, 3, at, :].astype(F32) + drecv[1, 3, at, :].astype(F32)
-        own[1, at, :] = total
-    dw[...] = own[1, :CHUNK, :].T.astype(BF16)
+        dw[at, :] = total.astype(BF16)
 
     for c in started:
         c.wait_send()
@@ -454,12 +459,27 @@
                 states[slot][1][d - 1].wait_send()
 
 
-def body(*args):
+def deliver_kernel(*refs):
+    for source, target in zip(refs[:4], refs[4:]):
+        target[...] = source[...]
+
+
+def deliver(results):
+    vmem = pl.BlockSpec(memory_space=pltpu.VMEM)
+    return pl.pallas_call(
+        deliver_kernel,
+        out_shape=tuple(jax.ShapeDtypeStruct(x.shape, x.dtype) for x in results),
+        in_specs=[vmem] * 4,
+        out_specs=(vmem,) * 4,
+    )(*results)
+
+
+def body(q, k, v, og, w):
     vmem = pl.BlockSpec(memory_space=pltpu.VMEM)
     block = jax.ShapeDtypeStruct((TOK, COLS), BF16)
-    return pl.pallas_call(
+    results = pl.pallas_call(
         kernel,
-        out_shape=(block, block, block, jax.ShapeDtypeStruct((COLS, CHUNK), BF16)),
+        out_shape=(block, block, block, jax.ShapeDtypeStruct((CHUNK, COLS), BF16)),
         in_specs=[vmem] * 4 + [pl.BlockSpec(memory_space=pl.ANY)],
         out_specs=(vmem,) * 4,
         scratch_shapes=[
@@ -489,6 +509,7 @@
             pltpu.VMEM((2, 4, CHUNK, COLS), BF16),
             pltpu.VMEM((256, NY * TOK), BF16),
             pltpu.VMEM((TOK, COLS), BF16),
+            pltpu.VMEM((2, 128, COLS), F32),
             pltpu.SemaphoreType.DMA((SEMS,)),
             pltpu.SemaphoreType.DMA((SEMS,)),
             pltpu.SemaphoreType.DMA((NZ,)),
@@ -496,16 +517,17 @@
         compiler_params=pltpu.CompilerParams(
             collective_id=0, has_side_effects=True, vmem_limit_bytes=56 << 20
         ),
-    )(*args)
+    )(q, k, v, w.T, og)
+    *grads, weight_grad = deliver(results)
+    return *grads, weight_grad.T
 
 
 def solution(mesh):
     placed = (P("seq", "tp"), P("seq", "tp"), P("seq", "tp"), P("seq", None), P("tp", "seq"))
-    inner = jax.shard_map(
-        lambda q, k, v, og, w: body(q, k, v, w, og),
+    return jax.shard_map(
+        body,
         mesh=mesh,
         in_specs=placed,
         out_specs=(P("seq", "tp"), P("seq", "tp"), P("seq", "tp"), P("tp", "seq")),
         check_vma=False,
     )
-    return inner

time: 122 us -> 99.1 us (0.81)
  Pallas kernels: 112 us -> 98.1 us
  local copies, waits for them, and re-layouts: 9.04 us -> 0 us
    pallas_call x1, Pallas kernels: 112 us -> 95.7 us  [body(): pl.pallas_call(kernel, out_shape=(block, block, block, jax.ShapeDtypeStru...]
    unnamed x4 -> x0, local copies, waits for them, and re-layouts: 7.18 us -> none
    pallas_call x0 -> x1, Pallas kernels: none -> 2.45 us  [deliver(): pl.pallas_call(deliver_kernel, out_shape=tuple((jax.ShapeDtypeStruct(x.sh...]
    pallas_call x1 -> x0, local copies, waits for them, and re-layouts: 1.87 us -> none  [body(): pl.pallas_call(kernel, out_shape=(block, block, block, jax.ShapeDtypeStru...]
where the time goes in v2:
time: 99.1 us; the launch traced here: 98.8 us
  Pallas kernels  98.1 us (99%)
    pallas_call x1, Pallas kernels, body(): pl.pallas_call(kernel, out_shape=(block, block, block, jax.ShapeDtypeStru...  95.7 us
    pallas_call x1, Pallas kernels, deliver(): pl.pallas_call(deliver_kernel, out_shape=tuple((jax.ShapeDtypeStruct(x.sh...  2.45 us

profile of v2, /device:TPU:2, one launch (start us, length us, event | category | flops | bytes accessed | tf_op | source)
XLA Modules:
  0.0 98.8 jit_solution(7876100084565017372)
XLA Ops:
  0.6 95.7 %shard_map.84 = (bf16[256,768]{1,0:T(8,128)(2,1)}, bf16[256,768]{1,0:T(8,128)(2,1)}, bf16[256,768]{1,0:T(8,128)(2,1)}, bf16[192,768]{1,0:T(8,128)(2,1)}) custom-call(bf16[256,768]{1,0:T(8,128)(2,1)} %q.1, bf16[256,768]{1,0:T(8,128)(2,1)} %k.1, bf16[256,768]{1,0:T(8,128)(2,1)} %v.1, bf16[192,768]{1,0:T(8,128)(2,1)} %bitcast.2, bf16[256,6144]{1,0:T(8,128)(2,1)} %og.1), custom_call_target="tpu_custom_call" | custom-call | tf_op jit(solution)/shard_map/pallas_call | solution.py:480
  96.3 2.4 %shard_map.85 = (bf16[256,768]{1,0:T(8,128)(2,1)}, bf16[256,768]{1,0:T(8,128)(2,1)}, bf16[256,768]{1,0:T(8,128)(2,1)}, bf16[192,768]{1,0:T(8,128)(2,1)}) custom-call(bf16[256,768]{1,0:T(8,128)(2,1)} %get-tuple-element.12.refs_0_, bf16[256,768]{1,0:T(8,128)(2,1)} %get-tuple-element.13.refs_1_, bf16[256,768]{1,0:T(8,128)(2,1)} %get-tuple-element.14.refs_2_, ...), custom_call_target="tpu_custom_call" | custom-call | tf_op jit(solution)/shard_map/pallas_call | solution.py:469

commit v3 on v2

--- a/solution.py
+++ b/solution.py
@@ -35,7 +35,7 @@
     q, k, v, w, og, qg, kg, vg, dw,
     grads, weights, normed, scores, att, ng, part, psend, precv, hsend, hrecv,
     lstate, lrecv, tsend, trecv, tacc, pfs, state, blocks, ssend, srecv,
-    own, dsend, drecv, turned, gh, held, send, recv, lsem,
+    own, dsend, drecv, turned, gh, held, raw, vsend, vrecv, send, recv, lsem,
 ):
     s, t = lax.axis_index("seq"), lax.axis_index("tp")
     z, y = s // NY, s % NY
@@ -130,14 +130,12 @@
         ):
             bcopy[r, name] = copy(piece(at_t, half), piece(at_t, half), s, tp)
 
-    def weight_step(step):
-        for turn in (0, 1):
-            for way in (0, 1):
-                h = way ^ turn
-                if (step, way, h) in wcopy:
-                    wcopy[step, way, h].wait_recv()
-                    if (step + 1, way, h) in wcopy:
-                        go(wcopy[step + 1, way, h])
+    def weight_half(step, turn):
+        for way in (0, 1):
+            h = way ^ turn
+            wcopy[step, way, h].wait_recv()
+            if (step + 1, way, h) in wcopy:
+                go(wcopy[step + 1, way, h])
 
     def local_state(a, b, slot):
         for g in range(2):
@@ -240,9 +238,8 @@
     local_state(k, v, 0)
     pl.semaphore_wait(barrier, len(peers))
     state_first(0)
-    for turn in (0, 1):
-        for way in (0, 1):
-            go(wcopy[0, way, way ^ turn])
+    for way in (0, 1):
+        go(wcopy[0, way, way])
     for d in range(1, NY):
         go(acopy[d])
 
@@ -262,22 +259,40 @@
             scores[4 * g + h] = score
             att[:, at] += dot(score, v[:, at] * mask, 1, 0)
 
+    ncopy = {
+        "up": copy(raw.at[pl.ds(0, TOK)], raw.at[pl.ds(3 * TOK, TOK)], along_y(1), t),
+        "down": copy(raw.at[pl.ds(0, TOK)], raw.at[pl.ds(TOK, TOK)], along_y(3), t),
+        "far_up": copy(
+            raw.at[pl.ds(3 * TOK, 128)], raw.at[pl.ds(2 * TOK, 128)], along_y(1), t
+        ),
+        "far_down": copy(
+            raw.at[pl.ds(TOK + 128, 128)], raw.at[pl.ds(2 * TOK + 128, 128)], along_y(3), t
+        ),
+    }
+    vcopy = [copy(vsend, vrecv.at[NY - d], along_y(d), t) for d in range(1, NY)]
+
     forward(0)
     state_second(0)
-    weight_step(0)
+    for way in (0, 1):
+        go(wcopy[0, way, 1 - way])
+    weight_half(0, 0)
     for d in range(1, NY):
         acopy[d].wait_recv()
         for name in ("right", "left", "twin"):
             go(bcopy[NY - d, name])
     forward(1)
+    weight_half(0, 1)
     state_third(0)
-    weight_step(1)
+    weight_half(1, 0)
     state_last(0)
     for g in range(2):
         at = lanes(g, 0, GROUP)
         att[:, at] += dot(q[:, at], blocks[0, g], 1, 0)
-    attended = att[...]
-    sum_send(0, jnp.sum(attended * attended, axis=1, keepdims=True))
+    raw[pl.ds(0, TOK), :] = att[...].astype(BF16)
+    go(ncopy["up"])
+    go(ncopy["down"])
+    sum_send(0, jnp.sum(att[...] * att[...], axis=1, keepdims=True))
+    weight_half(1, 1)
     for r in range(1, NY):
         bcopy[r, "right"].wait_recv()
         go(bcopy[r, "far_right"])
@@ -285,28 +300,22 @@
         bcopy[r, "left"].wait_recv()
         go(bcopy[r, "far_left"])
         go(bcopy[r, "twin_right"])
+    weight_half(2, 0)
     inverse = 1.0 / jnp.sqrt(sum_wait(0) / MODEL + EPSILON)
-    normed[pl.ds(0, TOK), :] = (att[...] * inverse).astype(BF16)
-
-    ncopy = {
-        "up": copy(normed.at[pl.ds(0, TOK)], normed.at[pl.ds(3 * TOK, TOK)], along_y(1), t),
-        "down": copy(normed.at[pl.ds(0, TOK)], normed.at[pl.ds(TOK, TOK)], along_y(3), t),
-        "far_up": copy(
-            normed.at[pl.ds(3 * TOK, 128)], normed.at[pl.ds(2 * TOK, 128)], along_y(1), t
-        ),
-        "far_down": copy(
-            normed.at[pl.ds(TOK + 128, 128)], normed.at[pl.ds(2 * TOK + 128, 128)], along_y(3), t
-        ),
-    }
-    go(ncopy["up"])
-    go(ncopy["down"])
-    weight_step(2)
+    vsend[...] = jnp.broadcast_to(inverse, (TOK, 128)).T[:8]
+    for c in vcopy:
+        go(c)
+    weight_half(2, 1)
+    ncopy["up"].wait_recv()
+    go(ncopy["far_up"])
+    ncopy["down"].wait_recv()
+    go(ncopy["far_down"])
     for r in range(1, NY):
         bcopy[r, "far_right"].wait_recv()
         go(bcopy[r, "twin_far0"])
         bcopy[r, "far_left"].wait_recv()
         go(bcopy[r, "twin_far1"])
-    weight_step(3)
+    weight_half(3, 0)
     for name in ("twin", "twin_left", "twin_right", "twin_far0", "twin_far1"):
         for r in range(1, NY):
             bcopy[r, name].wait_recv()
@@ -363,14 +372,23 @@
             dsend[way, step, HALF * h : HALF * (h + 1), :] = total.astype(BF16)
             go(dcopy[step, way, h])
 
-    ncopy["up"].wait_recv()
-    go(ncopy["far_up"])
-    ncopy["down"].wait_recv()
-    go(ncopy["far_down"])
     product(2)
     hsend[...] = part[...].astype(BF16)
     go(half_up)
     go(half_down)
+    ncopy["far_up"].wait_recv()
+    ncopy["far_down"].wait_recv()
+    for c in vcopy:
+        c.wait_recv()
+    for r in range(NY):
+        at = pl.ds(TOK * r, TOK)
+        if r == 0:
+            normed[at, :] = (att[...] * inverse).astype(BF16)
+        else:
+            scale = jnp.broadcast_to(vrecv[r, :1], (128, TOK)).T[:, :1]
+            normed[at, :] = (raw[at, :].astype(F32) * scale).astype(BF16)
+    chunk(4)
+    grad_half(0, 1)
     product(1)
     psend[0, 128:] = part[128:].astype(BF16)
     go(pcopy[0, 1])
@@ -379,10 +397,6 @@
     psend[1, :128] = part[:128].astype(BF16)
     go(pcopy[1, 0])
     held[1] = part[128:]
-    ncopy["far_up"].wait_recv()
-    ncopy["far_down"].wait_recv()
-    chunk(4)
-    grad_half(0, 1)
 
     @pl.loop(0, 2)
     def _(i):
@@ -398,10 +412,9 @@
     grad_half(1, 1)
     product(0)
 
-    @pl.loop(0, 5)
+    @pl.loop(0, 2)
     def _(i):
-        e = i % 2
-        chunk((1 - e) * ((6 + i // 2) % NZ) + e * (2 - i // 2))
+        chunk(6 - 4 * i)
 
     grad_half(2, 0)
     for c in pcopy.values():
@@ -409,6 +422,11 @@
     ng[...] = part[...] + precv[0].astype(F32) + precv[1].astype(F32)
     sum_send(1, jnp.sum(ng[...] * att[...], axis=1, keepdims=True))
     grad_half(2, 1)
+
+    @pl.loop(0, 3)
+    def _(i):
+        chunk((1 - i + NZ) % NZ)
+
     cross = sum_wait(1) * inverse
     grad_heads = (ng[...] - att[...] * (inverse * cross / MODEL)) * inverse
     gh[...] = grad_heads.astype(BF16)
@@ -510,6 +528,9 @@
             pltpu.VMEM((256, NY * TOK), BF16),
             pltpu.VMEM((TOK, COLS), BF16),
             pltpu.VMEM((2, 128, COLS), F32),
+            pltpu.VMEM((NY * TOK, COLS), BF16),
+            pltpu.VMEM((8, TOK), F32),
+            pltpu.VMEM((NY, 8, TOK), F32),
             pltpu.SemaphoreType.DMA((SEMS,)),
             pltpu.SemaphoreType.DMA((SEMS,)),
             pltpu.SemaphoreType.DMA((NZ,)),

time: 99.1 us -> 88.5 us (0.89)
  Pallas kernels: 98.1 us -> 87.4 us
    pallas_call x1, Pallas kernels: 95.7 us -> 85 us  [body(): pl.pallas_call(kernel, out_shape=(block, block, block, jax.ShapeDtypeStru...]
where the time goes in v3:
time: 88.5 us; the launch traced here: 88.1 us
  Pallas kernels  87.4 us (99%)
    pallas_call x1, Pallas kernels, body(): pl.pallas_call(kernel, out_shape=(block, block, block, jax.ShapeDtypeStru...  85 us
    pallas_call x1, Pallas kernels, deliver(): pl.pallas_call(deliver_kernel, out_shape=tuple((jax.ShapeDtypeStruct(x.sh...  2.45 us

profile of v3, /device:TPU:2, one launch (start us, length us, event | category | flops | bytes accessed | tf_op | source)
XLA Modules:
  0.0 88.1 jit_solution(16607704402373741755)
XLA Ops:
  0.6 85.0 %shard_map.84 = (bf16[256,768]{1,0:T(8,128)(2,1)}, bf16[256,768]{1,0:T(8,128)(2,1)}, bf16[256,768]{1,0:T(8,128)(2,1)}, bf16[192,768]{1,0:T(8,128)(2,1)}) custom-call(bf16[256,768]{1,0:T(8,128)(2,1)} %q.1, bf16[256,768]{1,0:T(8,128)(2,1)} %k.1, bf16[256,768]{1,0:T(8,128)(2,1)} %v.1, bf16[192,768]{1,0:T(8,128)(2,1)} %bitcast.2, bf16[256,6144]{1,0:T(8,128)(2,1)} %og.1), custom_call_target="tpu_custom_call" | custom-call | tf_op jit(solution)/shard_map/pallas_call | solution.py:498
  85.6 2.4 %shard_map.85 = (bf16[256,768]{1,0:T(8,128)(2,1)}, bf16[256,768]{1,0:T(8,128)(2,1)}, bf16[256,768]{1,0:T(8,128)(2,1)}, bf16[192,768]{1,0:T(8,128)(2,1)}) custom-call(bf16[256,768]{1,0:T(8,128)(2,1)} %get-tuple-element.12.refs_0_, bf16[256,768]{1,0:T(8,128)(2,1)} %get-tuple-element.13.refs_1_, bf16[256,768]{1,0:T(8,128)(2,1)} %get-tuple-element.14.refs_2_, ...), custom_call_target="tpu_custom_call" | custom-call | tf_op jit(solution)/shard_map/pallas_call | solution.py:487

commit v4 on v3

--- a/solution.py
+++ b/solution.py
@@ -34,7 +34,7 @@
 def kernel(
     q, k, v, w, og, qg, kg, vg, dw,
     grads, weights, normed, scores, att, ng, part, psend, precv, hsend, hrecv,
-    lstate, lrecv, tsend, trecv, tacc, pfs, state, blocks, ssend, srecv,
+    lstate, lrecv, tsend, trecv, bsend, brecv, tacc, pfs, state, blocks, ssend, srecv,
     own, dsend, drecv, turned, gh, held, raw, vsend, vrecv, send, recv, lsem,
 ):
     s, t = lax.axis_index("seq"), lax.axis_index("tp")
@@ -145,9 +145,11 @@
                 kept = kept + full[HDIM * h : HDIM * (h + 1), :] * head_mask(h, 0, GROUP)
             lstate[slot, HDIM * g : HDIM * (g + 1), :] = kept.astype(BF16)
 
+    place = z % 4
+    outward = jnp.where(place == 3, 1, -1)
+    at_edge = (place == 0) | (place == 3)
     states = []
     for slot in (0, 1):
-        sign = 1 - 2 * slot
         first = [
             copy(
                 lstate.at[slot, pl.ds(pl.multiple_of(QUARTER * ((y + d) % NY), 16), QUARTER)],
@@ -156,8 +158,10 @@
             for d in range(1, NY)
         ]
         second = [
-            copy(tsend.at[slot], trecv.at[slot, z], along_z(sign * d), t) for d in range(1, NZ)
+            copy(tsend.at[slot], trecv.at[slot, place], along_z((place + d) % 4 - place), t)
+            for d in range(1, 4)
         ]
+        edge = [copy(bsend.at[slot], brecv.at[slot], along_z(outward * d), t) for d in (1, 2)]
         third = [
             copy(
                 pfs.at[slot, (y + d) % NY],
@@ -166,7 +170,7 @@
             )
             for d in range(1, NY)
         ]
-        states.append((first, second, third))
+        states.append((first, second, third, edge))
 
     def state_first(slot):
         for c in states[slot][0]:
@@ -181,23 +185,34 @@
         for j in range(1, NY):
             total = total + lrecv[slot, j].astype(F32)
         tsend[slot] = total.astype(BF16)
-        for d in range(1, NZ):
-            reaches = z + d < NZ if slot == 0 else z >= d
-
-            @pl.when(reaches)
+        for c in states[slot][1]:
+            go(c)
+        trecv[slot, place] = tsend[slot]
+
+    def state_middle(slot):
+        for c in states[slot][1]:
+            c.wait_recv()
+        before, total = jnp.zeros((QUARTER, GROUP), F32), jnp.zeros((QUARTER, GROUP), F32)
+        for j in range(4):
+            plane = trecv[slot, j].astype(F32)
+            total = total + plane
+            counts = j < place if slot == 0 else j > place
+            before = before + jnp.where(counts, plane, 0.0)
+        tacc[...] = before
+        bsend[slot] = total.astype(BF16)
+
+        @pl.when(at_edge & (z // 4 == slot))
+        def _():
+            for c in states[slot][3]:
+                c.start()
+
+    def state_third(slot):
+        for i, near in enumerate((at_edge, jnp.logical_not(at_edge))):
+
+            @pl.when(near & (z // 4 == 1 - slot))
             def _():
-                states[slot][1][d - 1].start()
-
-    def state_third(slot):
-        tacc[...] = jnp.zeros((QUARTER, GROUP), F32)
-        for d in range(1, NZ):
-            comes = z >= d if slot == 0 else z + d < NZ
-            source = z - d if slot == 0 else z + d
-
-            @pl.when(comes)
-            def _():
-                states[slot][1][d - 1].wait_recv()
-                tacc[...] += trecv[slot, source].astype(F32)
+                states[slot][3][i].wait_recv()
+                tacc[...] += brecv[slot].astype(F32)
 
         running = tacc[...]
         for j in range(NY) if slot == 0 else reversed(range(NY)):
@@ -259,22 +274,33 @@
             scores[4 * g + h] = score
             att[:, at] += dot(score, v[:, at] * mask, 1, 0)
 
-    ncopy = {
-        "up": copy(raw.at[pl.ds(0, TOK)], raw.at[pl.ds(3 * TOK, TOK)], along_y(1), t),
-        "down": copy(raw.at[pl.ds(0, TOK)], raw.at[pl.ds(TOK, TOK)], along_y(3), t),
-        "far_up": copy(
-            raw.at[pl.ds(3 * TOK, 128)], raw.at[pl.ds(2 * TOK, 128)], along_y(1), t
-        ),
-        "far_down": copy(
-            raw.at[pl.ds(TOK + 128, 128)], raw.at[pl.ds(2 * TOK + 128, 128)], along_y(3), t
-        ),
-    }
+    ncopy = {}
+    for name, d, slot, first in (("up", 1, 3, 0), ("down", 3, 1, 1)):
+        for turn, h in enumerate((first, 1 - first)):
+            ncopy[name, turn] = copy(
+                raw.at[pl.ds(128 * h, 128)], raw.at[pl.ds(TOK * slot + 128 * h, 128)],
+                along_y(d), t,
+            )
+        ncopy[name, 2] = copy(
+            raw.at[pl.ds(TOK * slot + 128 * first, 128)],
+            raw.at[pl.ds(2 * TOK + 128 * first, 128)],
+            along_y(d), t,
+        )
     vcopy = [copy(vsend, vrecv.at[NY - d], along_y(d), t) for d in range(1, NY)]
+
+    def turn_window(at_t):
+        @pl.loop(1, NY)
+        def _(r):
+            block = grads[
+                pl.ds(pl.multiple_of(TOK * r, TOK), TOK), pl.ds(pl.multiple_of(256 * at_t, 256), 256)
+            ]
+            turned[at_t, :, pl.ds(pl.multiple_of(TOK * r, TOK), TOK)] = block.T
 
     forward(0)
     state_second(0)
     for way in (0, 1):
         go(wcopy[0, way, 1 - way])
+    state_middle(0)
     weight_half(0, 0)
     for d in range(1, NY):
         acopy[d].wait_recv()
@@ -282,6 +308,13 @@
             go(bcopy[NY - d, name])
     forward(1)
     weight_half(0, 1)
+    for c in own_grads:
+        c.wait()
+
+    @pl.loop(0, NZ)
+    def _(j):
+        turned[j, :, :TOK] = grads[:TOK, pl.ds(pl.multiple_of(256 * j, 256), 256)].T
+
     state_third(0)
     weight_half(1, 0)
     state_last(0)
@@ -289,8 +322,9 @@
         at = lanes(g, 0, GROUP)
         att[:, at] += dot(q[:, at], blocks[0, g], 1, 0)
     raw[pl.ds(0, TOK), :] = att[...].astype(BF16)
-    go(ncopy["up"])
-    go(ncopy["down"])
+    for turn in (0, 1):
+        for name in ("up", "down"):
+            go(ncopy[name, turn])
     sum_send(0, jnp.sum(att[...] * att[...], axis=1, keepdims=True))
     weight_half(1, 1)
     for r in range(1, NY):
@@ -300,27 +334,28 @@
         bcopy[r, "left"].wait_recv()
         go(bcopy[r, "far_left"])
         go(bcopy[r, "twin_right"])
+    for at_t in (t, right, left):
+        turn_window(at_t)
     weight_half(2, 0)
+    for name in ("up", "down"):
+        ncopy[name, 0].wait_recv()
+        go(ncopy[name, 2])
     inverse = 1.0 / jnp.sqrt(sum_wait(0) / MODEL + EPSILON)
     vsend[...] = jnp.broadcast_to(inverse, (TOK, 128)).T[:8]
     for c in vcopy:
         go(c)
     weight_half(2, 1)
-    ncopy["up"].wait_recv()
-    go(ncopy["far_up"])
-    ncopy["down"].wait_recv()
-    go(ncopy["far_down"])
     for r in range(1, NY):
         bcopy[r, "far_right"].wait_recv()
         go(bcopy[r, "twin_far0"])
         bcopy[r, "far_left"].wait_recv()
         go(bcopy[r, "twin_far1"])
-    weight_half(3, 0)
     for name in ("twin", "twin_left", "twin_right", "twin_far0", "twin_far1"):
         for r in range(1, NY):
             bcopy[r, name].wait_recv()
-    for c in own_grads:
-        c.wait()
+    for at_t in (twin, (twin + 2) % NT, (twin + 6) % NT, (t + 4) % NT, (twin + 4) % NT):
+        turn_window(at_t)
+    weight_half(3, 0)
 
     def product(r):
         @pl.loop(0, 3)
@@ -338,12 +373,11 @@
 
     def chunk(off):
         j = (z + off) % NZ
-        turned[...] = grads[:, pl.ds(pl.multiple_of(256 * j, 256), 256)].T
 
         @pl.loop(0, 3)
         def _(n):
             at = pl.ds(pl.multiple_of(256 * n, 256), 256)
-            own[off, :, at] = dot(turned[...], normed[:, at], 1, 0)
+            own[off, :, at] = dot(turned[j], normed[:, at], 1, 0)
 
     def valid(off, h):
         return own[off, pl.ds(pl.multiple_of(64 * odd + HALF * h, 32), HALF), :]
@@ -376,8 +410,9 @@
     hsend[...] = part[...].astype(BF16)
     go(half_up)
     go(half_down)
-    ncopy["far_up"].wait_recv()
-    ncopy["far_down"].wait_recv()
+    for name in ("up", "down"):
+        ncopy[name, 1].wait_recv()
+        ncopy[name, 2].wait_recv()
     for c in vcopy:
         c.wait_recv()
     for r in range(NY):
@@ -412,9 +447,10 @@
     grad_half(1, 1)
     product(0)
 
-    @pl.loop(0, 2)
+    @pl.loop(0, 5)
     def _(i):
-        chunk(6 - 4 * i)
+        e = i % 2
+        chunk((1 - e) * ((6 + i // 2) % NZ) + e * (2 - i // 2))
 
     grad_half(2, 0)
     for c in pcopy.values():
@@ -422,16 +458,12 @@
     ng[...] = part[...] + precv[0].astype(F32) + precv[1].astype(F32)
     sum_send(1, jnp.sum(ng[...] * att[...], axis=1, keepdims=True))
     grad_half(2, 1)
-
-    @pl.loop(0, 3)
-    def _(i):
-        chunk((1 - i + NZ) % NZ)
-
     cross = sum_wait(1) * inverse
     grad_heads = (ng[...] - att[...] * (inverse * cross / MODEL)) * inverse
     gh[...] = grad_heads.astype(BF16)
     local_state(q, gh, 1)
     state_first(1)
+    grad_half(3, 0)
 
     def backward(g):
         at = lanes(g, 0, GROUP)
@@ -449,11 +481,11 @@
 
     backward(0)
     state_second(1)
-    grad_half(3, 0)
+    state_middle(1)
+    grad_half(3, 1)
     backward(1)
     qg[...] = att[...].astype(BF16)
     state_third(1)
-    grad_half(3, 1)
     state_last(1)
     for g in range(2):
         at = lanes(g, 0, GROUP)
@@ -469,12 +501,11 @@
     for c in started:
         c.wait_send()
     for slot in (0, 1):
-        for d in range(1, NZ):
-            reaches = z + d < NZ if slot == 0 else z >= d
-
-            @pl.when(reaches)
-            def _():
-                states[slot][1][d - 1].wait_send()
+
+        @pl.when(at_edge & (z // 4 == slot))
+        def _():
+            for c in states[slot][3]:
+                c.wait_send()
 
 
 def deliver_kernel(*refs):
@@ -515,7 +546,9 @@
             pltpu.VMEM((2, 192, GROUP), BF16),
             pltpu.VMEM((2, NY, QUARTER, GROUP), BF16),
             pltpu.VMEM((2, QUARTER, GROUP), BF16),
-            pltpu.VMEM((2, NZ, QUARTER, GROUP), BF16),
+            pltpu.VMEM((2, 4, QUARTER, GROUP), BF16),
+            pltpu.VMEM((2, QUARTER, GROUP), BF16),
+            pltpu.VMEM((2, QUARTER, GROUP), BF16),
             pltpu.VMEM((QUARTER, GROUP), F32),
             pltpu.VMEM((2, NY, QUARTER, GROUP), BF16),
             pltpu.VMEM((2, 192, GROUP), BF16),
@@ -525,7 +558,7 @@
             pltpu.VMEM((NZ, 256, COLS), F32),
             pltpu.VMEM((2, 4, CHUNK, COLS), BF16),
             pltpu.VMEM((2, 4, CHUNK, COLS), BF16),
-            pltpu.VMEM((256, NY * TOK), BF16),
+            pltpu.VMEM((NZ, 256, NY * TOK), BF16),
             pltpu.VMEM((TOK, COLS), BF16),
             pltpu.VMEM((2, 128, COLS), F32),
             pltpu.VMEM((NY * TOK, COLS), BF16),

time: 88.5 us -> 87 us (0.983); the launches traced: 88.1 us -> 85.5 us
  Pallas kernels: 87.4 us -> 84.8 us
    pallas_call x1, Pallas kernels: 85 us -> 82.4 us  [body(): pl.pallas_call(kernel, out_shape=(block, block, block, jax.ShapeDtypeStru...]
where the time goes in v4:
time: 87 us; the launch traced here: 85.5 us
  Pallas kernels  84.8 us (97%)
    pallas_call x1, Pallas kernels, body(): pl.pallas_call(kernel, out_shape=(block, block, block, jax.ShapeDtypeStru...  82.4 us
    pallas_call x1, Pallas kernels, deliver(): pl.pallas_call(deliver_kernel, out_shape=tuple((jax.ShapeDtypeStruct(x.sh...  2.45 us

profile of v4, /device:TPU:2, one launch (start us, length us, event | category | flops | bytes accessed | tf_op | source)
XLA Modules:
  0.0 85.5 jit_solution(17959573833716048705)
XLA Ops:
  0.6 82.4 %shard_map.84 = (bf16[256,768]{1,0:T(8,128)(2,1)}, bf16[256,768]{1,0:T(8,128)(2,1)}, bf16[256,768]{1,0:T(8,128)(2,1)}, bf16[192,768]{1,0:T(8,128)(2,1)}) custom-call(bf16[256,768]{1,0:T(8,128)(2,1)} %q.1, bf16[256,768]{1,0:T(8,128)(2,1)} %k.1, bf16[256,768]{1,0:T(8,128)(2,1)} %v.1, bf16[192,768]{1,0:T(8,128)(2,1)} %bitcast.2, bf16[256,6144]{1,0:T(8,128)(2,1)} %og.1), custom_call_target="tpu_custom_call" | custom-call | tf_op jit(solution)/shard_map/pallas_call | solution.py:529
  83.0 2.4 %shard_map.85 = (bf16[256,768]{1,0:T(8,128)(2,1)}, bf16[256,768]{1,0:T(8,128)(2,1)}, bf16[256,768]{1,0:T(8,128)(2,1)}, bf16[192,768]{1,0:T(8,128)(2,1)}) custom-call(bf16[256,768]{1,0:T(8,128)(2,1)} %get-tuple-element.12.refs_0_, bf16[256,768]{1,0:T(8,128)(2,1)} %get-tuple-element.13.refs_1_, bf16[256,768]{1,0:T(8,128)(2,1)} %get-tuple-element.14.refs_2_, ...), custom_call_target="tpu_custom_call" | custom-call | tf_op jit(solution)/shard_map/pallas_call | solution.py:518

commit v5 on v4

--- a/solution.py
+++ b/solution.py
@@ -32,7 +32,8 @@
 
 
 def kernel(
-    q, k, v, w, og, qg, kg, vg, dw,
+    q_in, k_in, v_in, w_in, og, qg, kg, vg, dw,
+    q, k, v,
     grads, weights, normed, scores, att, ng, part, psend, precv, hsend, hrecv,
     lstate, lrecv, tsend, trecv, bsend, brecv, tacc, pfs, state, blocks, ssend, srecv,
     own, dsend, drecv, turned, gh, held, raw, vsend, vrecv, send, recv, lsem,
@@ -75,6 +76,17 @@
     def window(at_z, at_y):
         return pl.multiple_of(COLS * at_z + GROUP * (at_y // 2) + 128 * (at_y % 2), 128)
 
+    def weight_rows(j, h, n):
+        return pl.ds(pl.multiple_of(256 * j + 64 * odd + HALF * h, 32), n)
+
+    loads = [
+        pltpu.make_async_copy(source, target, lsem.at[NZ + i])
+        for i, (source, target) in enumerate(
+            ((w_in, weights.at[weight_rows(z, 0, CHUNK)]), (k_in, k), (v_in, v), (q_in, q))
+        )
+    ]
+    for c in loads:
+        c.start()
     own_grads = []
     for j in range(NZ):
         c = pltpu.make_async_copy(
@@ -88,11 +100,6 @@
     for j in range(NZ):
         pad = pl.multiple_of(256 * j + CHUNK * (1 - odd), 64)
         weights[pl.ds(pad, 64), :] = jnp.zeros((64, COLS), BF16)
-
-    def weight_rows(j, h, n):
-        return pl.ds(pl.multiple_of(256 * j + 64 * odd + HALF * h, 32), n)
-
-    weights[weight_rows(z, 0, CHUNK), :] = w[...]
 
     wcopy = {}
     for step in range(4):
@@ -250,6 +257,8 @@
             total = total + srecv[i, d - 1]
         return jnp.broadcast_to(total[:1], (128, TOK)).T[:, :1]
 
+    for c in loads:
+        c.wait()
     local_state(k, v, 0)
     pl.semaphore_wait(barrier, len(peers))
     state_first(0)
@@ -509,8 +518,12 @@
 
 
 def deliver_kernel(*refs):
-    for source, target in zip(refs[:4], refs[4:]):
-        target[...] = source[...]
+    sems = refs[-1]
+    copies = [pltpu.make_async_copy(refs[i], refs[4 + i], sems.at[i]) for i in range(4)]
+    for c in copies:
+        c.start()
+    for c in copies:
+        c.wait()
 
 
 def deliver(results):
@@ -519,19 +532,23 @@
         deliver_kernel,
         out_shape=tuple(jax.ShapeDtypeStruct(x.shape, x.dtype) for x in results),
         in_specs=[vmem] * 4,
-        out_specs=(vmem,) * 4,
+        out_specs=(pl.BlockSpec(memory_space=pl.ANY),) * 4,
+        scratch_shapes=[pltpu.SemaphoreType.DMA((4,))],
     )(*results)
 
 
 def body(q, k, v, og, w):
     vmem = pl.BlockSpec(memory_space=pltpu.VMEM)
-    block = jax.ShapeDtypeStruct((TOK, COLS), BF16)
+    block = pltpu.VMEM((TOK, COLS), BF16)
     results = pl.pallas_call(
         kernel,
-        out_shape=(block, block, block, jax.ShapeDtypeStruct((CHUNK, COLS), BF16)),
-        in_specs=[vmem] * 4 + [pl.BlockSpec(memory_space=pl.ANY)],
+        out_shape=(block, block, block, pltpu.VMEM((CHUNK, COLS), BF16)),
+        in_specs=[pl.BlockSpec(memory_space=pltpu.HBM)] * 5,
         out_specs=(vmem,) * 4,
         scratch_shapes=[
+            pltpu.VMEM((TOK, COLS), BF16),
+            pltpu.VMEM((TOK, COLS), BF16),
+            pltpu.VMEM((TOK, COLS), BF16),
             pltpu.VMEM((NY * TOK, NZ * 256), BF16),
             pltpu.VMEM((NZ * 256, COLS), BF16),
             pltpu.VMEM((NY * TOK, COLS), BF16),
@@ -566,13 +583,13 @@
             pltpu.VMEM((NY, 8, TOK), F32),
             pltpu.SemaphoreType.DMA((SEMS,)),
             pltpu.SemaphoreType.DMA((SEMS,)),
-            pltpu.SemaphoreType.DMA((NZ,)),
+            pltpu.SemaphoreType.DMA((NZ + 4,)),
         ],
         compiler_params=pltpu.CompilerParams(
             collective_id=0, has_side_effects=True, vmem_limit_bytes=56 << 20
         ),
     )(q, k, v, w.T, og)
-    *grads, weight_grad = deliver(results)
+    *grads, weight_grad = deliver([pltpu.with_memory_space_constraint(x, pltpu.VMEM) for x in results])
     return *grads, weight_grad.T
 
 

time: 87 us -> 83.4 us (0.959)
  Pallas kernels: 84.8 us -> 81.2 us
    pallas_call x1, Pallas kernels: 82.4 us -> 80.1 us  [body(): pl.pallas_call(kernel, out_shape=(block, block, block, pltpu.VMEM((CHUNK,...]
    pallas_call x1, Pallas kernels: 2.45 us -> 1.14 us  [deliver(): pl.pallas_call(deliver_kernel, out_shape=tuple((jax.ShapeDtypeStruct(x.sh...]
where the time goes in v5:
time: 83.4 us; the launch traced here: 81.9 us
  Pallas kernels  81.2 us (97%)
    pallas_call x1, Pallas kernels, body(): pl.pallas_call(kernel, out_shape=(block, block, block, pltpu.VMEM((CHUNK,...  80.1 us

profile of v5, /device:TPU:2, one launch (start us, length us, event | category | flops | bytes accessed | tf_op | source)
XLA Modules:
  0.0 81.9 jit_solution(35999561020296202)
XLA Ops:
  0.6 80.1 %shard_map.84 = (bf16[256,768]{1,0:T(8,128)(2,1)S(1)}, bf16[256,768]{1,0:T(8,128)(2,1)S(1)}, bf16[256,768]{1,0:T(8,128)(2,1)S(1)}, bf16[192,768]{1,0:T(8,128)(2,1)S(1)}) custom-call(bf16[256,768]{1,0:T(8,128)(2,1)} %q_in.1, bf16[256,768]{1,0:T(8,128)(2,1)} %k_in.1, bf16[256,768]{1,0:T(8,128)(2,1)} %v_in.1, bf16[192,768]{1,0:T(8,128)(2,1)} %bitcast.2, ...), custom_call_target="tpu_custom_call" | custom-call | tf_op jit(solution)/shard_map/pallas_call | solution.py:543
  80.7 1.1 %shard_map.85 = (bf16[256,768]{1,0:T(8,128)(2,1)}, bf16[256,768]{1,0:T(8,128)(2,1)}, bf16[256,768]{1,0:T(8,128)(2,1)}, bf16[192,768]{1,0:T(8,128)(2,1)}) custom-call(bf16[256,768]{1,0:T(8,128)(2,1)S(1)} %get-tuple-element.12.refs_0_, bf16[256,768]{1,0:T(8,128)(2,1)S(1)} %get-tuple-element.13.refs_1_, bf16[256,768]{1,0:T(8,128)(2,1)S(1)} %get-tuple-element.14.refs_2_, ...), custom_call_target="tpu_custom_call" | custom-call | tf_op jit(solution)/shard_map/pallas_call | solution.py:531

commit v6 on v5

--- a/solution.py
+++ b/solution.py
@@ -309,8 +309,8 @@
     state_second(0)
     for way in (0, 1):
         go(wcopy[0, way, 1 - way])
+    weight_half(0, 0)
     state_middle(0)
-    weight_half(0, 0)
     for d in range(1, NY):
         acopy[d].wait_recv()
         for name in ("right", "left", "twin"):
@@ -490,8 +490,8 @@
 
     backward(0)
     state_second(1)
+    grad_half(3, 1)
     state_middle(1)
-    grad_half(3, 1)
     backward(1)
     qg[...] = att[...].astype(BF16)
     state_third(1)

time: 83.4 us -> 82.7 us (level)
  no operation moved by 1% of the time
where the time goes in v6:
time: 82.7 us; the launch traced here: 81.7 us
  Pallas kernels  81 us (98%)
    pallas_call x1, Pallas kernels, body(): pl.pallas_call(kernel, out_shape=(block, block, block, pltpu.VMEM((CHUNK,...  79.9 us

profile of v6, /device:TPU:2, one launch (start us, length us, event | category | flops | bytes accessed | tf_op | source)
XLA Modules:
  0.0 81.7 jit_solution(7608430500013021741)
XLA Ops:
  0.6 79.9 %shard_map.84 = (bf16[256,768]{1,0:T(8,128)(2,1)S(1)}, bf16[256,768]{1,0:T(8,128)(2,1)S(1)}, bf16[256,768]{1,0:T(8,128)(2,1)S(1)}, bf16[192,768]{1,0:T(8,128)(2,1)S(1)}) custom-call(bf16[256,768]{1,0:T(8,128)(2,1)} %q_in.1, bf16[256,768]{1,0:T(8,128)(2,1)} %k_in.1, bf16[256,768]{1,0:T(8,128)(2,1)} %v_in.1, bf16[192,768]{1,0:T(8,128)(2,1)} %bitcast.2, ...), custom_call_target="tpu_custom_call" | custom-call | tf_op jit(solution)/shard_map/pallas_call | solution.py:543
  80.5 1.1 %shard_map.85 = (bf16[256,768]{1,0:T(8,128)(2,1)}, bf16[256,768]{1,0:T(8,128)(2,1)}, bf16[256,768]{1,0:T(8,128)(2,1)}, bf16[192,768]{1,0:T(8,128)(2,1)}) custom-call(bf16[256,768]{1,0:T(8,128)(2,1)S(1)} %get-tuple-element.12.refs_0_, bf16[256,768]{1,0:T(8,128)(2,1)S(1)} %get-tuple-element.13.refs_1_, bf16[256,768]{1,0:T(8,128)(2,1)S(1)} %get-tuple-element.14.refs_2_, ...), custom_call_target="tpu_custom_call" | custom-call | tf_op jit(solution)/shard_map/pallas_call | solution.py:531
